TPU v7x, 32 devices: a whole 2x2x4 slice. The times are simulated.
32 devices in a mesh: dir: 2 (over x), sx: 4 (over y, core), sy: 4 (over z).
Axes of the slice: x: 2, y: 2, z: 4, core: 2. Of those that a mesh axis runs over, the one named last changes fastest.
Arguments:
- signs_x: int32 [2, 256], P('dir', 'sx'), may hold values from -2147483648 to 2147483647, as said below
- signs_y: int32 [2, 512], P('dir', 'sy'), may hold values from -2147483648 to 2147483647, as said below
- heights: int32 [256, 512], P('sx', 'sy'), may hold values from 0 to 63
- velocity: float32 [256, 512], P('sx', 'sy'), may hold values from 1 to 2
- background: float32 [2, 256, 512], P('dir', 'sx', 'sy'), may hold values from -4 to 4
Outputs:
- basis: float32 [64, 256, 512], P('dir', 'sx', 'sy')
- factor: float32 [64, 64], P('dir')
Inputs may be any that keep to these rules, and one draw needn't show every extreme that they name: `signs_x`: packed sign words, every bit pattern possible. `signs_y`: packed sign words, every bit pattern possible.
All inputs are finite; a program needn't handle non-finite values.
Results may differ from a plain program's by a relative error of at most 0.00027.
Values sent between devices are 32-bit elements; how exact they have to be, the bound alone decides.
A program may use at most 64 MiB of HBM per device.

v0:
```python
import math
import jax
import jax.numpy as jnp
from jax import lax
from jax.sharding import PartitionSpec as P

PROBES = 32
LEVELS = 64
tau_step = 0.02


def with_halo(cells, sides, width):
    for axis, dim in sides:
        count = lax.axis_size(axis)
        ends = count - 1
        head = lax.slice_in_dim(cells, 0, width, axis=dim)
        tail = lax.slice_in_dim(cells, cells.shape[dim] - width, cells.shape[dim], axis=dim)
        cells = jnp.concatenate(
            [
                lax.ppermute(tail, axis, [(i, (i + 1) % count) for i in range(ends)]),
                cells,
                lax.ppermute(head, axis, [((i + 1) % count, i) for i in range(ends)]),
            ],
            axis=dim,
        )
    return cells


def unpack_signs(packed, per_group):
    bit_index = jnp.arange(per_group, dtype=jnp.int32)
    bit_values = jnp.right_shift(packed[:, None, :], bit_index[None, :, None]) & 1
    signed = (2 * bit_values - 1).astype(jnp.float32)
    return signed.reshape(packed.shape[0] * per_group, packed.shape[1])


def apply_step(wavefield, stiffness):
    weighted = stiffness * wavefield
    padded = with_halo(weighted, (("sx", 1), ("sy", 2)), 1)
    laplace = (
        padded[:, 2:, 1:-1]
        + padded[:, :-2, 1:-1]
        + padded[:, 1:-1, 2:]
        + padded[:, 1:-1, :-2]
        - 4.0 * weighted
    )
    return wavefield + tau_step * stiffness * laplace


def responses_for(signs_first, signs_second, shot_data, stiffness):
    first_signs = unpack_signs(signs_first, PROBES)
    second = unpack_signs(signs_second, PROBES)
    kronecker = first_signs[:, :, None] * second[:, None, :]
    groups = shot_data.shape[0]
    rows_x = shot_data.shape[1]
    rows_y = shot_data.shape[2]
    rolled = jnp.roll(kronecker.reshape(groups, PROBES, rows_x, rows_y), -1, axis=1).reshape(
        kronecker.shape
    )
    probe_dirs = kronecker + 0.5 * rolled
    shot_fields = jnp.repeat(shot_data, PROBES, axis=0)
    wavefield = shot_fields * probe_dirs
    for repeat in range(4):
        wavefield = apply_step(wavefield, stiffness[None])
    return (shot_fields * wavefield).reshape(groups * PROBES, rows_x * rows_y)


def shards(signs_x, signs_y, heights, velocity, background):
    rows_x = background.shape[1]
    rows_y = background.shape[2]
    stiffness = velocity * jnp.sqrt(1.0 + heights.astype(jnp.float32) / LEVELS)
    response = responses_for(signs_x, signs_y, background, stiffness)
    all_rows = lax.all_gather(response, "dir", axis=0, tiled=True)
    local_gram = jnp.dot(
        all_rows, all_rows.T, precision=lax.Precision.HIGHEST, preferred_element_type=jnp.float32
    )
    gram_matrix = lax.psum(local_gram, ("sx", "sy"))
    factor_low = jnp.linalg.cholesky(gram_matrix)
    orthonormal = lax.linalg.triangular_solve(factor_low, all_rows, left_side=True, lower=True)
    factor_r = factor_low.T
    cell_count = math.sqrt(rows_x * rows_y * lax.axis_size("sx") * lax.axis_size("sy"))
    row_start = lax.axis_index("dir") * PROBES
    own_q = lax.dynamic_slice_in_dim(orthonormal, row_start, PROBES, 0)
    own_r = lax.dynamic_slice_in_dim(factor_r, row_start, PROBES, 0)
    basis = (own_q * cell_count).reshape(PROBES, rows_x, rows_y)
    factor = own_r / cell_count
    return (basis, factor)


def solution(mesh):
    in_specs = (P("dir", "sx"), P("dir", "sy"), P("sx", "sy"), P("sx", "sy"), P("dir", "sx", "sy"))
    out_specs = (P("dir", "sx", "sy"), P("dir", None))
    return jax.shard_map(shards, mesh=mesh, in_specs=in_specs, out_specs=out_specs, check_vma=False)
```

profile of v0, /device:TPU:0, one launch (start us, length us, event | category | flops | bytes accessed | tf_op | source)
XLA Modules:
  0.0 231.4 jit_solution(7985730447501686642)
XLA Ops:
  10.2 1.3 collective-permute-start
  11.5 3.0 %collective-permute-start.1 = (f32[32,1,128]{2,0,1:T(8,128)S(1)}, f32[32,1,128]{2,0,1:T(8,128)S(1)}, u32[]{:S(2)}, u32[]{:S(2)}) collective-permute-start(f32[32,1,128]{2,0,1:T(8,128)S(1)} %get-tuple-element.34), channel_id=1, source_target_pairs={{0,4},{4,8},{8,12},{1,5},{5,9},{9,13},{2,6},{6,10},{10,14},{3,7},{... | collective-permute-start | bytes 49160 | tf_op jit(solution)/shard_map/ppermute | solution.py:20
  15.4 1.8 fusion.39
  17.1 1.9 copy.23
  20.3 1.9 copy.25
  22.2 5.6 %collective-permute-start.3 = (f32[32,66,1]{1,0,2:T(8,128)S(1)}, f32[32,66,1]{1,0,2:T(8,128)S(1)}, u32[]{:S(2)}, u32[]{:S(2)}) collective-permute-start(f32[32,66,1]{1,0,2:T(8,128)S(1)} %copy.25), channel_id=1, source_target_pairs={{0,1},{1,2},{2,3},{4,5},{5,6},{6,7},{8,9},{9,10},{10,11},{12,13},{... | collective-permute-start | bytes 25352 | tf_op jit(solution)/shard_map/ppermute | solution.py:20
  27.7 1.9 copy.24
  29.6 1.9 copy.26
  31.6 3.9 %broadcast_multiply_fusion.2 = (f32[32,64,128]{2,0,1:T(8,128)S(1)}, f32[32,64,128]{2,0,1:T(8,128)}) fusion(f32[64,128]{1,0:T(8,128)S(1)} %get-tuple-element.19, f32[32,64,128]{2,0,1:T(8,128)S(1)} %fusion.29, f32[32,1,128]{2,0,1:T(8,128)S(1)} %collective-permute-done, f32[32,1,128]{2,0,1:T(8,128)S(1)} %collective-permute-done.1, f32[32,66,1]{2,0,1:T(8,128)} %copy.26, ...), kind=kLoop, calls=%fused_computation.71 | loop fusion | flops 5505024 | bytes 4366848 | tf_op jit(solution)/shard_map/mul | solution.py:37
  36.8 3.6 %collective-permute-start.5 = (f32[32,1,128]{2,0,1:T(8,128)S(1)}, f32[32,1,128]{2,0,1:T(8,128)S(1)}, u32[]{:S(2)}, u32[]{:S(2)}) collective-permute-start(f32[32,1,128]{2,0,1:T(8,128)S(1)} %get-tuple-element.32), channel_id=1, source_target_pairs={{0,4},{4,8},{8,12},{1,5},{5,9},{9,13},{2,6},{6,10},{10,14},{3,7},{... | collective-permute-start | bytes 49160 | tf_op jit(solution)/shard_map/ppermute | solution.py:20
  41.2 1.4 fusion.38
  42.6 1.9 copy.27
  46.5 4.5 %collective-permute-start.7 = (f32[32,66,1]{1,0,2:T(8,128)S(1)}, f32[32,66,1]{1,0,2:T(8,128)S(1)}, u32[]{:S(2)}, u32[]{:S(2)}) collective-permute-start(f32[32,66,1]{1,0,2:T(8,128)S(1)} %copy.29), channel_id=1, source_target_pairs={{0,1},{1,2},{2,3},{4,5},{5,6},{6,7},{8,9},{9,10},{10,11},{12,13},{... | collective-permute-start | bytes 25352 | tf_op jit(solution)/shard_map/ppermute | solution.py:20
  52.5 1.9 copy.30
  54.4 3.4 %broadcast_multiply_fusion.1 = (f32[32,64,128]{2,0,1:T(8,128)S(1)}, f32[32,64,128]{2,0,1:T(8,128)}) fusion(f32[64,128]{1,0:T(8,128)S(1)} %get-tuple-element.19, f32[32,64,128]{2,0,1:T(8,128)} %get-tuple-element.17, f32[32,64,128]{2,0,1:T(8,128)S(1)} %get-tuple-element.16, f32[32,1,128]{2,0,1:T(8,128)S(1)} %collective-permute-done.4, ...), kind=kLoop, calls=%fused_computation.70 | loop fusion | flops 4194304 | bytes 4309504 | tf_op jit(solution)/shard_map/mul | solution.py:37
  59.1 4.6 %collective-permute-start.9 = (f32[32,1,128]{2,0,1:T(8,128)S(1)}, f32[32,1,128]{2,0,1:T(8,128)S(1)}, u32[]{:S(2)}, u32[]{:S(2)}) collective-permute-start(f32[32,1,128]{2,0,1:T(8,128)S(1)} %get-tuple-element.30), channel_id=1, source_target_pairs={{0,4},{4,8},{8,12},{1,5},{5,9},{9,13},{2,6},{6,10},{10,14},{3,7},{... | collective-permute-start | bytes 49160 | tf_op jit(solution)/shard_map/ppermute | solution.py:20
  65.7 1.3 collective-permute-start.10
  67.7 4.7 %collective-permute-start.11 = (f32[32,66,1]{1,0,2:T(8,128)S(1)}, f32[32,66,1]{1,0,2:T(8,128)S(1)}, u32[]{:S(2)}, u32[]{:S(2)}) collective-permute-start(f32[32,66,1]{1,0,2:T(8,128)S(1)} %copy.33), channel_id=1, source_target_pairs={{0,1},{1,2},{2,3},{4,5},{5,6},{6,7},{8,9},{9,10},{10,11},{12,13},{... | collective-permute-start | bytes 25352 | tf_op jit(solution)/shard_map/ppermute | solution.py:20
  73.7 1.9 copy.34
  75.6 3.4 %broadcast_multiply_fusion = (f32[32,64,128]{2,0,1:T(8,128)S(1)}, f32[32,64,128]{2,0,1:T(8,128)}) fusion(f32[64,128]{1,0:T(8,128)S(1)} %get-tuple-element.19, f32[32,64,128]{2,0,1:T(8,128)} %get-tuple-element.15, f32[32,64,128]{2,0,1:T(8,128)S(1)} %get-tuple-element.14, f32[32,1,128]{2,0,1:T(8,128)S(1)} %collective-permute-done.8, ...), kind=kLoop, calls=%fused_computation.69 | loop fusion | flops 4194304 | bytes 4309504 | tf_op jit(solution)/shard_map/mul | solution.py:37
  80.3 5.5 %collective-permute-start.13 = (f32[32,1,128]{2,0,1:T(8,128)S(1)}, f32[32,1,128]{2,0,1:T(8,128)S(1)}, u32[]{:S(2)}, u32[]{:S(2)}) collective-permute-start(f32[32,1,128]{2,0,1:T(8,128)S(1)} %get-tuple-element.28), channel_id=1, source_target_pairs={{0,4},{4,8},{8,12},{1,5},{5,9},{9,13},{2,6},{6,10},{10,14},{3,7},{... | collective-permute-start | bytes 49160 | tf_op jit(solution)/shard_map/ppermute | solution.py:20
  86.7 1.4 fusion.36
  88.1 1.9 copy.35
  91.9 4.7 %collective-permute-start.15 = (f32[32,66,1]{1,0,2:T(8,128)S(1)}, f32[32,66,1]{1,0,2:T(8,128)S(1)}, u32[]{:S(2)}, u32[]{:S(2)}) collective-permute-start(f32[32,66,1]{1,0,2:T(8,128)S(1)} %copy.37), channel_id=1, source_target_pairs={{0,1},{1,2},{2,3},{4,5},{5,6},{6,7},{8,9},{9,10},{10,11},{12,13},{... | collective-permute-start | bytes 25352 | tf_op jit(solution)/shard_map/ppermute | solution.py:20
  98.1 1.9 copy.38
  100.0 3.1 %copy_bitcast_fusion = f32[32,8192]{1,0:T(8,128)} fusion(f32[32,64,128]{2,0,1:T(8,128)S(1)} %copy-done.1, f32[32,66,1]{2,0,1:T(8,128)} %copy.38, f32[32,1,128]{2,0,1:T(8,128)S(1)} %collective-permute-done.12, f32[32,64,128]{2,0,1:T(8,128)S(1)} %get-tuple-element.12, f32[32,1,128]{2,0,1:T(8,128)S(1)} %collective-permute-done.13, f32[32,66,1]{2,0,1:T(8,128)S(1)} %copy.36, ...), kind=kLoop, calls=%fused_computation.4 | loop fusion | flops 4194304 | bytes 3260928 | tf_op jit(solution)/shard_map/reshape | solution.py:64
  103.1 39.8 %all-gather.2.cloned.1.call-done = f32[64,8192]{1,0:T(8,128)} async-done(((f32[32,8192]{1,0:T(8,128)}), f32[64,8192]{1,0:T(8,128)}) %all-gather.2.cloned.1.call-update) | async-done | bytes 2097168 | tf_op jit(solution)/shard_map/all_gather | solution.py:72
  142.9 4.2 %fusion.44 = f32[64,64]{0,1:T(8,128)S(1)} fusion(f32[64,8192]{1,0:T(8,128)} %all-gather.2.cloned.1.call-done), kind=kOutput, calls=%fused_computation.96 | convolution fusion | flops 402653184 | bytes 2113536 | tf_op jit(solution)/shard_map/dot_general | solution.py:73
  147.1 61.3 %psum.7 = f32[64,64]{0,1:T(8,128)S(1)} all-reduce(f32[64,64]{0,1:T(8,128)S(1)} %fusion.44), channel_id=1, replica_groups=mesh['dir'=2,'sx'=4,'sy'=4] {'sx','sy'}, use_global_device_ids=true, to_apply=%region_0.1 | all-reduce | flops 4096 | bytes 32768 | tf_op jit(solution)/shard_map/psum | solution.py:76
  208.5 5.8 %cholesky.16 = f32[64,64]{1,0:T(8,128)S(1)} custom-call(f32[64,64]{1,0:T(8,128)S(1)} %fusion.32), custom_call_target="Cholesky" | custom-call | tf_op jit(solution)/shard_map/jit(cholesky)/cholesky | solution.py:77
  215.7 4.9 %custom-call.6 = f32[1,64,64]{1,2,0:T(8,128)S(1)} custom-call(f32[1,64,64]{2,1,0:T(8,128)S(1)} %get-tuple-element.10), custom_call_target="InvertDiagBlocksLowerTriangular" | custom-call | tf_op jit(solution)/shard_map/triangular_solve | solution.py:78
  220.6 1.9 fusion.30
  (66 shorter events, 24.9 us)
Async XLA Ops:
  7.2 135.7 %all-gather.2.cloned.1.call-start = ((), (), s32[]{:S(2)}) async-start(), calls=%async_computation | async-start | bytes 3145728 | tf_op jit(solution)/shard_map/all_gather | solution.py:72
  9.0 0.8 copy-start.3
  9.0 0.8 copy-start.4
  9.0 0.8 copy-start.2
  10.2 4.3 %collective-permute-start = (f32[32,1,128]{2,0,1:T(8,128)S(1)}, f32[32,1,128]{2,0,1:T(8,128)S(1)}, u32[]{:S(2)}, u32[]{:S(2)}) collective-permute-start(f32[32,1,128]{2,0,1:T(8,128)S(1)} %get-tuple-element.35), channel_id=1, source_target_pairs={{4,0},{8,4},{12,8},{5,1},{9,5},{13,9},{6,2},{10,6},{14,10},{7,3},{... | collective-permute-start | bytes 49160 | tf_op jit(solution)/shard_map/ppermute | solution.py:22
  11.5 3.9 %collective-permute-start.1 = (f32[32,1,128]{2,0,1:T(8,128)S(1)}, f32[32,1,128]{2,0,1:T(8,128)S(1)}, u32[]{:S(2)}, u32[]{:S(2)}) collective-permute-start(f32[32,1,128]{2,0,1:T(8,128)S(1)} %get-tuple-element.34), channel_id=1, source_target_pairs={{0,4},{4,8},{8,12},{1,5},{5,9},{9,13},{2,6},{6,10},{10,14},{3,7},{... | collective-permute-start | bytes 49160 | tf_op jit(solution)/shard_map/ppermute | solution.py:20
  19.0 8.7 %collective-permute-start.2 = (f32[32,66,1]{1,0,2:T(8,128)S(1)}, f32[32,66,1]{1,0,2:T(8,128)S(1)}, u32[]{:S(2)}, u32[]{:S(2)}) collective-permute-start(f32[32,66,1]{1,0,2:T(8,128)S(1)} %copy.23), channel_id=1, source_target_pairs={{1,0},{2,1},{3,2},{5,4},{6,5},{7,6},{9,8},{10,9},{11,10},{13,12},{... | collective-permute-start | bytes 25352 | tf_op jit(solution)/shard_map/ppermute | solution.py:22
  22.2 7.5 %collective-permute-start.3 = (f32[32,66,1]{1,0,2:T(8,128)S(1)}, f32[32,66,1]{1,0,2:T(8,128)S(1)}, u32[]{:S(2)}, u32[]{:S(2)}) collective-permute-start(f32[32,66,1]{1,0,2:T(8,128)S(1)} %copy.25), channel_id=1, source_target_pairs={{0,1},{1,2},{2,3},{4,5},{5,6},{6,7},{8,9},{9,10},{10,11},{12,13},{... | collective-permute-start | bytes 25352 | tf_op jit(solution)/shard_map/ppermute | solution.py:20
  35.5 4.9 %collective-permute-start.4 = (f32[32,1,128]{2,0,1:T(8,128)S(1)}, f32[32,1,128]{2,0,1:T(8,128)S(1)}, u32[]{:S(2)}, u32[]{:S(2)}) collective-permute-start(f32[32,1,128]{2,0,1:T(8,128)S(1)} %get-tuple-element.33), channel_id=1, source_target_pairs={{4,0},{8,4},{12,8},{5,1},{9,5},{13,9},{6,2},{10,6},{14,10},{7,3},{... | collective-permute-start | bytes 49160 | tf_op jit(solution)/shard_map/ppermute | solution.py:22
  36.8 4.4 %collective-permute-start.5 = (f32[32,1,128]{2,0,1:T(8,128)S(1)}, f32[32,1,128]{2,0,1:T(8,128)S(1)}, u32[]{:S(2)}, u32[]{:S(2)}) collective-permute-start(f32[32,1,128]{2,0,1:T(8,128)S(1)} %get-tuple-element.32), channel_id=1, source_target_pairs={{0,4},{4,8},{8,12},{1,5},{5,9},{9,13},{2,6},{6,10},{10,14},{3,7},{... | collective-permute-start | bytes 49160 | tf_op jit(solution)/shard_map/ppermute | solution.py:20
  44.5 6.6 %collective-permute-start.6 = (f32[32,66,1]{1,0,2:T(8,128)S(1)}, f32[32,66,1]{1,0,2:T(8,128)S(1)}, u32[]{:S(2)}, u32[]{:S(2)}) collective-permute-start(f32[32,66,1]{1,0,2:T(8,128)S(1)} %copy.27), channel_id=1, source_target_pairs={{1,0},{2,1},{3,2},{5,4},{6,5},{7,6},{9,8},{10,9},{11,10},{13,12},{... | collective-permute-start | bytes 25352 | tf_op jit(solution)/shard_map/ppermute | solution.py:22
  46.5 6.0 %collective-permute-start.7 = (f32[32,66,1]{1,0,2:T(8,128)S(1)}, f32[32,66,1]{1,0,2:T(8,128)S(1)}, u32[]{:S(2)}, u32[]{:S(2)}) collective-permute-start(f32[32,66,1]{1,0,2:T(8,128)S(1)} %copy.29), channel_id=1, source_target_pairs={{0,1},{1,2},{2,3},{4,5},{5,6},{6,7},{8,9},{9,10},{10,11},{12,13},{... | collective-permute-start | bytes 25352 | tf_op jit(solution)/shard_map/ppermute | solution.py:20
  57.8 5.9 %collective-permute-start.8 = (f32[32,1,128]{2,0,1:T(8,128)S(1)}, f32[32,1,128]{2,0,1:T(8,128)S(1)}, u32[]{:S(2)}, u32[]{:S(2)}) collective-permute-start(f32[32,1,128]{2,0,1:T(8,128)S(1)} %get-tuple-element.31), channel_id=1, source_target_pairs={{4,0},{8,4},{12,8},{5,1},{9,5},{13,9},{6,2},{10,6},{14,10},{7,3},{... | collective-permute-start | bytes 49160 | tf_op jit(solution)/shard_map/ppermute | solution.py:22
  59.1 5.4 %collective-permute-start.9 = (f32[32,1,128]{2,0,1:T(8,128)S(1)}, f32[32,1,128]{2,0,1:T(8,128)S(1)}, u32[]{:S(2)}, u32[]{:S(2)}) collective-permute-start(f32[32,1,128]{2,0,1:T(8,128)S(1)} %get-tuple-element.30), channel_id=1, source_target_pairs={{0,4},{4,8},{8,12},{1,5},{5,9},{9,13},{2,6},{6,10},{10,14},{3,7},{... | collective-permute-start | bytes 49160 | tf_op jit(solution)/shard_map/ppermute | solution.py:20
  65.7 6.7 %collective-permute-start.10 = (f32[32,66,1]{1,0,2:T(8,128)S(1)}, f32[32,66,1]{1,0,2:T(8,128)S(1)}, u32[]{:S(2)}, u32[]{:S(2)}) collective-permute-start(f32[32,66,1]{1,0,2:T(8,128)S(1)} %copy.31), channel_id=1, source_target_pairs={{1,0},{2,1},{3,2},{5,4},{6,5},{7,6},{9,8},{10,9},{11,10},{13,12},{... | collective-permute-start | bytes 25352 | tf_op jit(solution)/shard_map/ppermute | solution.py:22
  67.7 6.0 %collective-permute-start.11 = (f32[32,66,1]{1,0,2:T(8,128)S(1)}, f32[32,66,1]{1,0,2:T(8,128)S(1)}, u32[]{:S(2)}, u32[]{:S(2)}) collective-permute-start(f32[32,66,1]{1,0,2:T(8,128)S(1)} %copy.33), channel_id=1, source_target_pairs={{0,1},{1,2},{2,3},{4,5},{5,6},{6,7},{8,9},{9,10},{10,11},{12,13},{... | collective-permute-start | bytes 25352 | tf_op jit(solution)/shard_map/ppermute | solution.py:20
  79.0 6.8 %collective-permute-start.12 = (f32[32,1,128]{2,0,1:T(8,128)S(1)}, f32[32,1,128]{2,0,1:T(8,128)S(1)}, u32[]{:S(2)}, u32[]{:S(2)}) collective-permute-start(f32[32,1,128]{2,0,1:T(8,128)S(1)} %get-tuple-element.29), channel_id=1, source_target_pairs={{4,0},{8,4},{12,8},{5,1},{9,5},{13,9},{6,2},{10,6},{14,10},{7,3},{... | collective-permute-start | bytes 49160 | tf_op jit(solution)/shard_map/ppermute | solution.py:22
  80.3 6.4 %collective-permute-start.13 = (f32[32,1,128]{2,0,1:T(8,128)S(1)}, f32[32,1,128]{2,0,1:T(8,128)S(1)}, u32[]{:S(2)}, u32[]{:S(2)}) collective-permute-start(f32[32,1,128]{2,0,1:T(8,128)S(1)} %get-tuple-element.28), channel_id=1, source_target_pairs={{0,4},{4,8},{8,12},{1,5},{5,9},{9,13},{2,6},{6,10},{10,14},{3,7},{... | collective-permute-start | bytes 49160 | tf_op jit(solution)/shard_map/ppermute | solution.py:20
  89.9 6.7 %collective-permute-start.14 = (f32[32,66,1]{1,0,2:T(8,128)S(1)}, f32[32,66,1]{1,0,2:T(8,128)S(1)}, u32[]{:S(2)}, u32[]{:S(2)}) collective-permute-start(f32[32,66,1]{1,0,2:T(8,128)S(1)} %copy.35), channel_id=1, source_target_pairs={{1,0},{2,1},{3,2},{5,4},{6,5},{7,6},{9,8},{10,9},{11,10},{13,12},{... | collective-permute-start | bytes 25352 | tf_op jit(solution)/shard_map/ppermute | solution.py:22
  91.9 8.0 %copy-start.1 = (f32[32,64,128]{2,0,1:T(8,128)S(1)}, f32[32,64,128]{2,0,1:T(8,128)}, u32[]{:S(2)}) copy-start(f32[32,64,128]{2,0,1:T(8,128)} %get-tuple-element.13) | copy-start | bytes 3145732
  91.9 6.1 %collective-permute-start.15 = (f32[32,66,1]{1,0,2:T(8,128)S(1)}, f32[32,66,1]{1,0,2:T(8,128)S(1)}, u32[]{:S(2)}, u32[]{:S(2)}) collective-permute-start(f32[32,66,1]{1,0,2:T(8,128)S(1)} %copy.37), channel_id=1, source_target_pairs={{0,1},{1,2},{2,3},{4,5},{5,6},{6,7},{8,9},{9,10},{10,11},{12,13},{... | collective-permute-start | bytes 25352 | tf_op jit(solution)/shard_map/ppermute | solution.py:20
  142.9 77.7 %copy-start = (f32[64,8192]{1,0:T(8,128)S(1)}, f32[64,8192]{1,0:T(8,128)}, u32[]{:S(2)}) copy-start(f32[64,8192]{1,0:T(8,128)} %all-gather.2.cloned.1.call-done) | copy-start | bytes 6291460
Sparse Core Ops, SparseCore 0:
  103.2 39.6 all-gather.1
where the time goes:
time: 232 us; the launch traced here: 231 us
  blocking collectives  61.3 us (26%)
  starting transfers between devices  46.5 us (20%)
  waiting for transfers between devices  43.9 us (19%)
  local copies, waits for them, and re-layouts  30.7 us (13%)
  other arithmetic  28.4 us (12%)
  between operations  14.4 us (6%)
  matrix products  6.09 us (3%)
    psum x1, blocking collectives, shards(): gram_matrix = lax.psum(local_gram, ('sx', 'sy'))  61.3 us
    all_gather x1, waiting for transfers between devices, shards(): all_rows = lax.all_gather(response, 'dir', axis=0, tiled=True)  39.8 us
    ppermute x8, starting transfers between devices, with_halo(): lax.ppermute(tail, axis, [(i, (i + 1) % count) for i in range(ends)])  36.2 us
    slice x8, local copies, waits for them, and re-layouts, with_halo(): head = lax.slice_in_dim(cells, 0, width, axis=dim)  11.2 us
    mul x4, other arithmetic, apply_step(): weighted = stiffness * wavefield  11 us
    ppermute x8, starting transfers between devices, with_halo(): lax.ppermute(head, axis, [((i + 1) % count, i) for i in range(ends)])  10.3 us
    ppermute x4, local copies, waits for them, and re-layouts, with_halo(): lax.ppermute(tail, axis, [(i, (i + 1) % count) for i in range(ends)])  7.68 us
    another operation x3, other arithmetic, shards(): factor_low = jnp.linalg.cholesky(gram_matrix)  6.52 us
  transfers between devices with their start and end apart: 17, of which 8 were waited for; matrix products, arithmetic and copies ran while one was open for 4% of the time, Pallas kernels for 0%

commit v1 on v0

--- a/solution.py
+++ b/solution.py
@@ -73,7 +73,10 @@
     local_gram = jnp.dot(
         all_rows, all_rows.T, precision=lax.Precision.HIGHEST, preferred_element_type=jnp.float32
     )
-    gram_matrix = lax.psum(local_gram, ("sx", "sy"))
+    render_the_pools = lambda content, mesh_name: jnp.sum(
+        lax.all_gather(content, mesh_name), axis=0
+    )
+    gram_matrix = render_the_pools(local_gram, ("sx", "sy"))
     factor_low = jnp.linalg.cholesky(gram_matrix)
     orthonormal = lax.linalg.triangular_solve(factor_low, all_rows, left_side=True, lower=True)
     factor_r = factor_low.T

time: 232 us -> 208 us (0.90)
  blocking collectives: 61.3 us -> 37.1 us
    psum x1 -> x0, blocking collectives: 61.3 us -> none  [shards(): gram_matrix = lax.psum(local_gram, ('sx', 'sy'))]
    all_gather x0 -> x1, blocking collectives: none -> 37.1 us  [shards(): lax.all_gather(content, mesh_name)]
where the time goes in v1:
time: 208 us; the launch traced here: 207 us
  starting transfers between devices  46.5 us (22%)
  waiting for transfers between devices  43.9 us (21%)
  blocking collectives  37.1 us (18%)
  local copies, waits for them, and re-layouts  30.7 us (15%)
  other arithmetic  28.5 us (14%)
  between operations  14.4 us (7%)
  matrix products  6.08 us (3%)
    all_gather x1, waiting for transfers between devices, shards(): all_rows = lax.all_gather(response, 'dir', axis=0, tiled=True)  39.8 us
    all_gather x1, blocking collectives, shards(): lax.all_gather(content, mesh_name)  37.1 us
    ppermute x8, starting transfers between devices, with_halo(): lax.ppermute(tail, axis, [(i, (i + 1) % count) for i in range(ends)])  36.2 us
    slice x8, local copies, waits for them, and re-layouts, with_halo(): head = lax.slice_in_dim(cells, 0, width, axis=dim)  11.2 us
    mul x4, other arithmetic, apply_step(): weighted = stiffness * wavefield  11 us
    ppermute x8, starting transfers between devices, with_halo(): lax.ppermute(head, axis, [((i + 1) % count, i) for i in range(ends)])  10.3 us
    ppermute x4, local copies, waits for them, and re-layouts, with_halo(): lax.ppermute(tail, axis, [(i, (i + 1) % count) for i in range(ends)])  7.68 us
    another operation x3, other arithmetic, shards(): factor_low = jnp.linalg.cholesky(gram_matrix)  6.52 us
  transfers between devices with their start and end apart: 17, of which 8 were waited for; matrix products, arithmetic and copies ran while one was open for 4% of the time, Pallas kernels for 0%

profile of v1, /device:TPU:0, one launch (start us, length us, event | category | flops | bytes accessed | tf_op | source)
XLA Modules:
  0.0 207.1 jit_solution(2844370236228669173)
XLA Ops:
  10.2 1.3 collective-permute-start
  11.5 3.0 %collective-permute-start.1 = (f32[32,1,128]{2,0,1:T(8,128)S(1)}, f32[32,1,128]{2,0,1:T(8,128)S(1)}, u32[]{:S(2)}, u32[]{:S(2)}) collective-permute-start(f32[32,1,128]{2,0,1:T(8,128)S(1)} %get-tuple-element.34), channel_id=1, source_target_pairs={{0,4},{4,8},{8,12},{1,5},{5,9},{9,13},{2,6},{6,10},{10,14},{3,7},{... | collective-permute-start | bytes 49160 | tf_op jit(solution)/shard_map/ppermute | solution.py:20
  15.4 1.8 fusion.39
  17.1 1.9 copy.20
  20.3 1.9 copy.22
  22.2 5.6 %collective-permute-start.3 = (f32[32,66,1]{1,0,2:T(8,128)S(1)}, f32[32,66,1]{1,0,2:T(8,128)S(1)}, u32[]{:S(2)}, u32[]{:S(2)}) collective-permute-start(f32[32,66,1]{1,0,2:T(8,128)S(1)} %copy.22), channel_id=1, source_target_pairs={{0,1},{1,2},{2,3},{4,5},{5,6},{6,7},{8,9},{9,10},{10,11},{12,13},{... | collective-permute-start | bytes 25352 | tf_op jit(solution)/shard_map/ppermute | solution.py:20
  27.7 1.9 copy.21
  29.6 1.9 copy.23
  31.6 3.9 %broadcast_multiply_fusion.2 = (f32[32,64,128]{2,0,1:T(8,128)S(1)}, f32[32,64,128]{2,0,1:T(8,128)}) fusion(f32[64,128]{1,0:T(8,128)S(1)} %get-tuple-element.19, f32[32,64,128]{2,0,1:T(8,128)S(1)} %fusion.29, f32[32,1,128]{2,0,1:T(8,128)S(1)} %collective-permute-done, f32[32,1,128]{2,0,1:T(8,128)S(1)} %collective-permute-done.1, f32[32,66,1]{2,0,1:T(8,128)} %copy.23, ...), kind=kLoop, calls=%fused_computation.71 | loop fusion | flops 5505024 | bytes 4366848 | tf_op jit(solution)/shard_map/mul | solution.py:37
  36.8 3.6 %collective-permute-start.5 = (f32[32,1,128]{2,0,1:T(8,128)S(1)}, f32[32,1,128]{2,0,1:T(8,128)S(1)}, u32[]{:S(2)}, u32[]{:S(2)}) collective-permute-start(f32[32,1,128]{2,0,1:T(8,128)S(1)} %get-tuple-element.32), channel_id=1, source_target_pairs={{0,4},{4,8},{8,12},{1,5},{5,9},{9,13},{2,6},{6,10},{10,14},{3,7},{... | collective-permute-start | bytes 49160 | tf_op jit(solution)/shard_map/ppermute | solution.py:20
  41.2 1.4 fusion.38
  42.6 1.9 copy.24
  46.5 4.5 %collective-permute-start.7 = (f32[32,66,1]{1,0,2:T(8,128)S(1)}, f32[32,66,1]{1,0,2:T(8,128)S(1)}, u32[]{:S(2)}, u32[]{:S(2)}) collective-permute-start(f32[32,66,1]{1,0,2:T(8,128)S(1)} %copy.26), channel_id=1, source_target_pairs={{0,1},{1,2},{2,3},{4,5},{5,6},{6,7},{8,9},{9,10},{10,11},{12,13},{... | collective-permute-start | bytes 25352 | tf_op jit(solution)/shard_map/ppermute | solution.py:20
  52.5 1.9 copy.27
  54.4 3.4 %broadcast_multiply_fusion.1 = (f32[32,64,128]{2,0,1:T(8,128)S(1)}, f32[32,64,128]{2,0,1:T(8,128)}) fusion(f32[64,128]{1,0:T(8,128)S(1)} %get-tuple-element.19, f32[32,64,128]{2,0,1:T(8,128)} %get-tuple-element.17, f32[32,64,128]{2,0,1:T(8,128)S(1)} %get-tuple-element.16, f32[32,1,128]{2,0,1:T(8,128)S(1)} %collective-permute-done.4, ...), kind=kLoop, calls=%fused_computation.70 | loop fusion | flops 4194304 | bytes 4309504 | tf_op jit(solution)/shard_map/mul | solution.py:37
  59.1 4.6 %collective-permute-start.9 = (f32[32,1,128]{2,0,1:T(8,128)S(1)}, f32[32,1,128]{2,0,1:T(8,128)S(1)}, u32[]{:S(2)}, u32[]{:S(2)}) collective-permute-start(f32[32,1,128]{2,0,1:T(8,128)S(1)} %get-tuple-element.30), channel_id=1, source_target_pairs={{0,4},{4,8},{8,12},{1,5},{5,9},{9,13},{2,6},{6,10},{10,14},{3,7},{... | collective-permute-start | bytes 49160 | tf_op jit(solution)/shard_map/ppermute | solution.py:20
  65.7 1.3 collective-permute-start.10
  67.7 4.7 %collective-permute-start.11 = (f32[32,66,1]{1,0,2:T(8,128)S(1)}, f32[32,66,1]{1,0,2:T(8,128)S(1)}, u32[]{:S(2)}, u32[]{:S(2)}) collective-permute-start(f32[32,66,1]{1,0,2:T(8,128)S(1)} %copy.30), channel_id=1, source_target_pairs={{0,1},{1,2},{2,3},{4,5},{5,6},{6,7},{8,9},{9,10},{10,11},{12,13},{... | collective-permute-start | bytes 25352 | tf_op jit(solution)/shard_map/ppermute | solution.py:20
  73.7 1.9 copy.31
  75.6 3.4 %broadcast_multiply_fusion = (f32[32,64,128]{2,0,1:T(8,128)S(1)}, f32[32,64,128]{2,0,1:T(8,128)}) fusion(f32[64,128]{1,0:T(8,128)S(1)} %get-tuple-element.19, f32[32,64,128]{2,0,1:T(8,128)} %get-tuple-element.15, f32[32,64,128]{2,0,1:T(8,128)S(1)} %get-tuple-element.14, f32[32,1,128]{2,0,1:T(8,128)S(1)} %collective-permute-done.8, ...), kind=kLoop, calls=%fused_computation.69 | loop fusion | flops 4194304 | bytes 4309504 | tf_op jit(solution)/shard_map/mul | solution.py:37
  80.3 5.5 %collective-permute-start.13 = (f32[32,1,128]{2,0,1:T(8,128)S(1)}, f32[32,1,128]{2,0,1:T(8,128)S(1)}, u32[]{:S(2)}, u32[]{:S(2)}) collective-permute-start(f32[32,1,128]{2,0,1:T(8,128)S(1)} %get-tuple-element.28), channel_id=1, source_target_pairs={{0,4},{4,8},{8,12},{1,5},{5,9},{9,13},{2,6},{6,10},{10,14},{3,7},{... | collective-permute-start | bytes 49160 | tf_op jit(solution)/shard_map/ppermute | solution.py:20
  86.7 1.4 fusion.36
  88.1 1.9 copy.32
  91.9 4.7 %collective-permute-start.15 = (f32[32,66,1]{1,0,2:T(8,128)S(1)}, f32[32,66,1]{1,0,2:T(8,128)S(1)}, u32[]{:S(2)}, u32[]{:S(2)}) collective-permute-start(f32[32,66,1]{1,0,2:T(8,128)S(1)} %copy.34), channel_id=1, source_target_pairs={{0,1},{1,2},{2,3},{4,5},{5,6},{6,7},{8,9},{9,10},{10,11},{12,13},{... | collective-permute-start | bytes 25352 | tf_op jit(solution)/shard_map/ppermute | solution.py:20
  98.1 1.9 copy.35
  100.0 3.1 %copy_bitcast_fusion = f32[32,8192]{1,0:T(8,128)} fusion(f32[32,64,128]{2,0,1:T(8,128)S(1)} %copy-done.1, f32[32,66,1]{2,0,1:T(8,128)} %copy.35, f32[32,1,128]{2,0,1:T(8,128)S(1)} %collective-permute-done.12, f32[32,64,128]{2,0,1:T(8,128)S(1)} %get-tuple-element.12, f32[32,1,128]{2,0,1:T(8,128)S(1)} %collective-permute-done.13, f32[32,66,1]{2,0,1:T(8,128)S(1)} %copy.33, ...), kind=kLoop, calls=%fused_computation.4 | loop fusion | flops 4194304 | bytes 3260928 | tf_op jit(solution)/shard_map/reshape | solution.py:64
  103.1 39.8 %all-gather.3.cloned.1.call-done = f32[64,8192]{1,0:T(8,128)} async-done(((f32[32,8192]{1,0:T(8,128)}), f32[64,8192]{1,0:T(8,128)}) %all-gather.3.cloned.1.call-update) | async-done | bytes 2097168 | tf_op jit(solution)/shard_map/all_gather | solution.py:72
  142.9 4.2 %fusion.44 = f32[64,64]{1,0:T(8,128)S(1)} fusion(f32[64,8192]{1,0:T(8,128)} %all-gather.3.cloned.1.call-done), kind=kOutput, calls=%fused_computation.96 | convolution fusion | flops 402653184 | bytes 2113536 | tf_op jit(solution)/shard_map/dot_general | solution.py:73
  147.0 37.1 %all-gather = f32[1024,64]{1,0:T(8,128)S(1)} all-gather(f32[64,64]{1,0:T(8,128)S(1)} %fusion.44), channel_id=2, replica_groups=mesh['dir'=2,'sx'=4,'sy'=4] {'sx','sy'}, dimensions={0}, use_global_device_ids=true | all-gather | bytes 278528 | tf_op jit(solution)/shard_map/all_gather | solution.py:77
  184.2 5.8 %cholesky.16 = f32[64,64]{1,0:T(8,128)S(1)} custom-call(f32[64,64]{1,0:T(8,128)S(1)} %fusion.32), custom_call_target="Cholesky" | custom-call | tf_op jit(solution)/shard_map/jit(cholesky)/cholesky | solution.py:80
  191.4 4.9 %custom-call.6 = f32[1,64,64]{1,2,0:T(8,128)S(1)} custom-call(f32[1,64,64]{2,1,0:T(8,128)S(1)} %get-tuple-element.10), custom_call_target="InvertDiagBlocksLowerTriangular" | custom-call | tf_op jit(solution)/shard_map/triangular_solve | solution.py:81
  196.4 1.9 fusion.30
  (67 shorter events, 25.0 us)
Async XLA Ops:
  7.2 135.7 %all-gather.3.cloned.1.call-start = ((), (), s32[]{:S(2)}) async-start(), calls=%async_computation | async-start | bytes 3145728 | tf_op jit(solution)/shard_map/all_gather | solution.py:72
  9.0 0.8 copy-start.3
  9.0 0.8 copy-start.4
  9.0 0.8 copy-start.2
  10.2 4.3 %collective-permute-start = (f32[32,1,128]{2,0,1:T(8,128)S(1)}, f32[32,1,128]{2,0,1:T(8,128)S(1)}, u32[]{:S(2)}, u32[]{:S(2)}) collective-permute-start(f32[32,1,128]{2,0,1:T(8,128)S(1)} %get-tuple-element.35), channel_id=1, source_target_pairs={{4,0},{8,4},{12,8},{5,1},{9,5},{13,9},{6,2},{10,6},{14,10},{7,3},{... | collective-permute-start | bytes 49160 | tf_op jit(solution)/shard_map/ppermute | solution.py:22
  11.5 3.9 %collective-permute-start.1 = (f32[32,1,128]{2,0,1:T(8,128)S(1)}, f32[32,1,128]{2,0,1:T(8,128)S(1)}, u32[]{:S(2)}, u32[]{:S(2)}) collective-permute-start(f32[32,1,128]{2,0,1:T(8,128)S(1)} %get-tuple-element.34), channel_id=1, source_target_pairs={{0,4},{4,8},{8,12},{1,5},{5,9},{9,13},{2,6},{6,10},{10,14},{3,7},{... | collective-permute-start | bytes 49160 | tf_op jit(solution)/shard_map/ppermute | solution.py:20
  19.0 8.7 %collective-permute-start.2 = (f32[32,66,1]{1,0,2:T(8,128)S(1)}, f32[32,66,1]{1,0,2:T(8,128)S(1)}, u32[]{:S(2)}, u32[]{:S(2)}) collective-permute-start(f32[32,66,1]{1,0,2:T(8,128)S(1)} %copy.20), channel_id=1, source_target_pairs={{1,0},{2,1},{3,2},{5,4},{6,5},{7,6},{9,8},{10,9},{11,10},{13,12},{... | collective-permute-start | bytes 25352 | tf_op jit(solution)/shard_map/ppermute | solution.py:22
  22.2 7.5 %collective-permute-start.3 = (f32[32,66,1]{1,0,2:T(8,128)S(1)}, f32[32,66,1]{1,0,2:T(8,128)S(1)}, u32[]{:S(2)}, u32[]{:S(2)}) collective-permute-start(f32[32,66,1]{1,0,2:T(8,128)S(1)} %copy.22), channel_id=1, source_target_pairs={{0,1},{1,2},{2,3},{4,5},{5,6},{6,7},{8,9},{9,10},{10,11},{12,13},{... | collective-permute-start | bytes 25352 | tf_op jit(solution)/shard_map/ppermute | solution.py:20
  35.5 4.9 %collective-permute-start.4 = (f32[32,1,128]{2,0,1:T(8,128)S(1)}, f32[32,1,128]{2,0,1:T(8,128)S(1)}, u32[]{:S(2)}, u32[]{:S(2)}) collective-permute-start(f32[32,1,128]{2,0,1:T(8,128)S(1)} %get-tuple-element.33), channel_id=1, source_target_pairs={{4,0},{8,4},{12,8},{5,1},{9,5},{13,9},{6,2},{10,6},{14,10},{7,3},{... | collective-permute-start | bytes 49160 | tf_op jit(solution)/shard_map/ppermute | solution.py:22
  36.8 4.4 %collective-permute-start.5 = (f32[32,1,128]{2,0,1:T(8,128)S(1)}, f32[32,1,128]{2,0,1:T(8,128)S(1)}, u32[]{:S(2)}, u32[]{:S(2)}) collective-permute-start(f32[32,1,128]{2,0,1:T(8,128)S(1)} %get-tuple-element.32), channel_id=1, source_target_pairs={{0,4},{4,8},{8,12},{1,5},{5,9},{9,13},{2,6},{6,10},{10,14},{3,7},{... | collective-permute-start | bytes 49160 | tf_op jit(solution)/shard_map/ppermute | solution.py:20
  44.5 6.6 %collective-permute-start.6 = (f32[32,66,1]{1,0,2:T(8,128)S(1)}, f32[32,66,1]{1,0,2:T(8,128)S(1)}, u32[]{:S(2)}, u32[]{:S(2)}) collective-permute-start(f32[32,66,1]{1,0,2:T(8,128)S(1)} %copy.24), channel_id=1, source_target_pairs={{1,0},{2,1},{3,2},{5,4},{6,5},{7,6},{9,8},{10,9},{11,10},{13,12},{... | collective-permute-start | bytes 25352 | tf_op jit(solution)/shard_map/ppermute | solution.py:22
  46.5 6.0 %collective-permute-start.7 = (f32[32,66,1]{1,0,2:T(8,128)S(1)}, f32[32,66,1]{1,0,2:T(8,128)S(1)}, u32[]{:S(2)}, u32[]{:S(2)}) collective-permute-start(f32[32,66,1]{1,0,2:T(8,128)S(1)} %copy.26), channel_id=1, source_target_pairs={{0,1},{1,2},{2,3},{4,5},{5,6},{6,7},{8,9},{9,10},{10,11},{12,13},{... | collective-permute-start | bytes 25352 | tf_op jit(solution)/shard_map/ppermute | solution.py:20
  57.8 5.9 %collective-permute-start.8 = (f32[32,1,128]{2,0,1:T(8,128)S(1)}, f32[32,1,128]{2,0,1:T(8,128)S(1)}, u32[]{:S(2)}, u32[]{:S(2)}) collective-permute-start(f32[32,1,128]{2,0,1:T(8,128)S(1)} %get-tuple-element.31), channel_id=1, source_target_pairs={{4,0},{8,4},{12,8},{5,1},{9,5},{13,9},{6,2},{10,6},{14,10},{7,3},{... | collective-permute-start | bytes 49160 | tf_op jit(solution)/shard_map/ppermute | solution.py:22
  59.1 5.4 %collective-permute-start.9 = (f32[32,1,128]{2,0,1:T(8,128)S(1)}, f32[32,1,128]{2,0,1:T(8,128)S(1)}, u32[]{:S(2)}, u32[]{:S(2)}) collective-permute-start(f32[32,1,128]{2,0,1:T(8,128)S(1)} %get-tuple-element.30), channel_id=1, source_target_pairs={{0,4},{4,8},{8,12},{1,5},{5,9},{9,13},{2,6},{6,10},{10,14},{3,7},{... | collective-permute-start | bytes 49160 | tf_op jit(solution)/shard_map/ppermute | solution.py:20
  65.7 6.7 %collective-permute-start.10 = (f32[32,66,1]{1,0,2:T(8,128)S(1)}, f32[32,66,1]{1,0,2:T(8,128)S(1)}, u32[]{:S(2)}, u32[]{:S(2)}) collective-permute-start(f32[32,66,1]{1,0,2:T(8,128)S(1)} %copy.28), channel_id=1, source_target_pairs={{1,0},{2,1},{3,2},{5,4},{6,5},{7,6},{9,8},{10,9},{11,10},{13,12},{... | collective-permute-start | bytes 25352 | tf_op jit(solution)/shard_map/ppermute | solution.py:22
  67.7 6.0 %collective-permute-start.11 = (f32[32,66,1]{1,0,2:T(8,128)S(1)}, f32[32,66,1]{1,0,2:T(8,128)S(1)}, u32[]{:S(2)}, u32[]{:S(2)}) collective-permute-start(f32[32,66,1]{1,0,2:T(8,128)S(1)} %copy.30), channel_id=1, source_target_pairs={{0,1},{1,2},{2,3},{4,5},{5,6},{6,7},{8,9},{9,10},{10,11},{12,13},{... | collective-permute-start | bytes 25352 | tf_op jit(solution)/shard_map/ppermute | solution.py:20
  79.0 6.8 %collective-permute-start.12 = (f32[32,1,128]{2,0,1:T(8,128)S(1)}, f32[32,1,128]{2,0,1:T(8,128)S(1)}, u32[]{:S(2)}, u32[]{:S(2)}) collective-permute-start(f32[32,1,128]{2,0,1:T(8,128)S(1)} %get-tuple-element.29), channel_id=1, source_target_pairs={{4,0},{8,4},{12,8},{5,1},{9,5},{13,9},{6,2},{10,6},{14,10},{7,3},{... | collective-permute-start | bytes 49160 | tf_op jit(solution)/shard_map/ppermute | solution.py:22
  80.3 6.4 %collective-permute-start.13 = (f32[32,1,128]{2,0,1:T(8,128)S(1)}, f32[32,1,128]{2,0,1:T(8,128)S(1)}, u32[]{:S(2)}, u32[]{:S(2)}) collective-permute-start(f32[32,1,128]{2,0,1:T(8,128)S(1)} %get-tuple-element.28), channel_id=1, source_target_pairs={{0,4},{4,8},{8,12},{1,5},{5,9},{9,13},{2,6},{6,10},{10,14},{3,7},{... | collective-permute-start | bytes 49160 | tf_op jit(solution)/shard_map/ppermute | solution.py:20
  89.9 6.7 %collective-permute-start.14 = (f32[32,66,1]{1,0,2:T(8,128)S(1)}, f32[32,66,1]{1,0,2:T(8,128)S(1)}, u32[]{:S(2)}, u32[]{:S(2)}) collective-permute-start(f32[32,66,1]{1,0,2:T(8,128)S(1)} %copy.32), channel_id=1, source_target_pairs={{1,0},{2,1},{3,2},{5,4},{6,5},{7,6},{9,8},{10,9},{11,10},{13,12},{... | collective-permute-start | bytes 25352 | tf_op jit(solution)/shard_map/ppermute | solution.py:22
  91.9 8.0 %copy-start.1 = (f32[32,64,128]{2,0,1:T(8,128)S(1)}, f32[32,64,128]{2,0,1:T(8,128)}, u32[]{:S(2)}) copy-start(f32[32,64,128]{2,0,1:T(8,128)} %get-tuple-element.13) | copy-start | bytes 3145732
  91.9 6.1 %collective-permute-start.15 = (f32[32,66,1]{1,0,2:T(8,128)S(1)}, f32[32,66,1]{1,0,2:T(8,128)S(1)}, u32[]{:S(2)}, u32[]{:S(2)}) collective-permute-start(f32[32,66,1]{1,0,2:T(8,128)S(1)} %copy.34), channel_id=1, source_target_pairs={{0,1},{1,2},{2,3},{4,5},{5,6},{6,7},{8,9},{9,10},{10,11},{12,13},{... | collective-permute-start | bytes 25352 | tf_op jit(solution)/shard_map/ppermute | solution.py:20
  142.9 53.5 %copy-start = (f32[64,8192]{1,0:T(8,128)S(1)}, f32[64,8192]{1,0:T(8,128)}, u32[]{:S(2)}) copy-start(f32[64,8192]{1,0:T(8,128)} %all-gather.3.cloned.1.call-done) | copy-start | bytes 6291460
Sparse Core Ops, SparseCore 0:
  103.2 39.6 all-gather.2
